TPU v7x, 32 devices: a whole 2x2x4 slice. The times are simulated.
32 devices in a mesh: group: 2 (over x), wide: 16 (over z, y, core).
Axes of the slice: x: 2, y: 2, z: 4, core: 2. Of those that a mesh axis runs over, the one named last changes fastest.
Arguments:
- tokens: bfloat16 [192, 2688], P('group', 'wide'), parts along dimension 0, may hold values from -6 to 6
- mix_gain: bfloat16 [2688], replicated, may hold values from 0.099609375 to 1.8984375
- proj_inner: bfloat16 [2688, 2, 4096], P(None, None, 'wide'), may hold values from -0.125 to 0.125
- proj_maps: bfloat16 [2688, 2048], P(None, 'wide'), may hold values from -0.125 to 0.125
- proj_step: bfloat16 [2688, 64], P(None, 'wide'), may hold values from -0.125 to 0.125
- window_inner: bfloat16 [192, 3, 4096], P('group', None, 'wide'), parts along dimension 0, may hold values from -6 to 6
- window_maps: bfloat16 [192, 3, 2048], P('group', None, 'wide'), parts along dimension 0, may hold values from -6 to 6
- kernel_inner: bfloat16 [4, 4096], P(None, 'wide'), may hold values from -3 to 3
- kernel_maps: bfloat16 [4, 2048], P(None, 'wide'), may hold values from -3 to 3
- step_bias: float32 [64], P('wide'), may hold values from -4 to -1
- decay_log: float32 [64], P('wide'), may hold values from -1 to 2.5
- skip_gain: float32 [64], P('wide'), may hold values from 0.5 to 2
- gated_gain: bfloat16 [4096], P('wide'), may hold values from 0.099609375 to 1.8984375
- proj_out: bfloat16 [4096, 2688], P('wide'), may hold values from -0.125 to 0.125
- ssm_state: float32 [192, 64, 64, 128], P('group', 'wide'), parts along dimension 0, may hold values from -0.6 to 0.6
- moe_gain: bfloat16 [2688], replicated, may hold values from 0.099609375 to 1.8984375
- router_weight: bfloat16 [2688, 16], replicated, may hold values from -0.125 to 0.125
- expert_ids: int32 [192, 6], P('group'), parts along dimension 0, may hold values from 0 to 15, all different within a row; in each aligned block of 96 rows (0 to 95, 96 to 191, ...) at most 96 rows name the same one
- expert_up: bfloat16 [16, 2688, 928], P('wide'), may hold values from -0.125 to 0.125
- expert_down: bfloat16 [16, 928, 2688], P('wide'), may hold values from -0.1875 to 0.1875
Outputs:
- next_hidden: bfloat16 [192, 2688], P('group', 'wide'), parts along dimension 0
- new_state: float32 [192, 64, 64, 128], P('group', 'wide'), parts along dimension 0
There are 2 independent parts, one for each index of `group`. A program takes and returns all parts, laid end to end along the dimension named above; an argument that names none is the same for every part. Nothing has to cross between parts.
Inputs may be any that keep to these rules, and one draw needn't show every extreme that they name: `expert_ids`: each token names 6 different experts; no expert is named by more than 96 tokens of a part, a bound that some block reaches.
All inputs are finite; a program needn't handle non-finite values.
Results may differ from a plain program's by a relative error of at most 0.013.
Values may be sent and summed in bfloat16 or wider, within the bound.
A program may use at most 128 MiB of HBM per device.

v0:
```python
import jax
import jax.numpy as jnp
from jax import lax
from jax.sharding import PartitionSpec as P

WIDTH = 2688
HEADS = 64
HEAD_DIM = 64
STATE = 128
GROUPS = 8
TOPK = 6
INNER = 4096
epsilon = 1e-05


def rms_scale(values, axis):
    return lax.rsqrt(jnp.mean(values * values, axis=axis, keepdims=True) + epsilon)


def convolve(window, fresh, kernel):
    stacked = jnp.concatenate([window, fresh[:, None, :]], axis=1).astype(jnp.float32)
    mixed = jnp.sum(stacked * kernel.astype(jnp.float32)[None], axis=1)
    return jax.nn.silu(mixed).astype(jnp.bfloat16)


def expert_rows(rows, upward, downward):
    hidden_units = jnp.dot(rows, upward, preferred_element_type=jnp.float32)
    active = jnp.square(jnp.maximum(hidden_units, 0.0)).astype(jnp.bfloat16)
    return jnp.dot(active, downward, preferred_element_type=jnp.float32).astype(jnp.bfloat16)


def route_gates(logits, expert_ids):
    onehot = (
        expert_ids[:, :, None] == jnp.arange(logits.shape[1], dtype=jnp.int32)[None, None, :]
    ).astype(jnp.float32)
    chosen = jnp.sum(onehot * logits[:, None, :], axis=2)
    score = jax.nn.sigmoid(chosen)
    return score / jnp.sum(score, axis=1, keepdims=True)


def slot_codes(expert_ids, experts, capacity):
    flat = expert_ids.reshape(-1)
    onehot = (flat[:, None] == jnp.arange(experts, dtype=jnp.int32)[None, :]).astype(jnp.int32)
    before = jnp.cumsum(onehot, axis=0) - onehot
    slots = jnp.sum(before * onehot, axis=1)
    return (flat * capacity + slots).reshape(expert_ids.shape)


def slot_tables(codes, gates, count):
    targets = jnp.arange(count, dtype=jnp.int32)
    match = codes[None, :, :] == targets[:, None, None]
    pick = jnp.any(match, axis=2).astype(jnp.bfloat16)
    weigh = jnp.sum(jnp.where(match, gates[None], 0.0), axis=2)
    return (pick, weigh)


def local(
    tokens,
    mix_gain,
    proj_inner,
    proj_maps,
    proj_step,
    window_inner,
    window_maps,
    kernel_inner,
    kernel_maps,
    step_bias,
    decay_log,
    skip_gain,
    gated_gain,
    proj_out,
    ssm_state,
    moe_gain,
    router_weight,
    expert_ids,
    expert_up,
    expert_down,
):
    devices = lax.axis_size("wide")
    device = lax.axis_index("wide")
    seqs = tokens.shape[0]
    slice_width = tokens.shape[1]
    capacity = min(seqs, 4 * seqs * TOPK // devices)
    full_tokens = lax.all_gather(tokens, "wide", axis=1, tiled=True)
    tokens_float = full_tokens.astype(jnp.float32)
    normed = (tokens_float * rms_scale(tokens_float, 1) * mix_gain.astype(jnp.float32)).astype(
        jnp.bfloat16
    )
    local_inner = proj_inner.shape[2]
    inner = jnp.dot(
        normed, proj_inner.reshape(WIDTH, 2 * local_inner), preferred_element_type=jnp.float32
    ).astype(jnp.bfloat16)
    gate_input = inner[:, :local_inner]
    raw_inner = inner[:, local_inner:]
    maps_raw = jnp.dot(normed, proj_maps, preferred_element_type=jnp.float32).astype(jnp.bfloat16)
    step_raw = jnp.dot(normed, proj_step, preferred_element_type=jnp.float32).astype(jnp.bfloat16)
    conv_inner = convolve(window_inner, raw_inner, kernel_inner)
    conv_maps = convolve(window_maps, maps_raw, kernel_maps)
    all_maps = lax.all_gather(conv_maps, "wide", axis=1, tiled=True)
    local_heads = proj_step.shape[1]
    group = device * local_heads // (HEADS // GROUPS)
    in_maps = lax.dynamic_slice_in_dim(all_maps, group * STATE, STATE, 1).astype(jnp.float32)
    out_maps = lax.dynamic_slice_in_dim(all_maps, GROUPS * STATE + group * STATE, STATE, 1).astype(
        jnp.float32
    )
    step_size = jax.nn.softplus(step_raw.astype(jnp.float32) + step_bias)
    decay = jnp.exp(-jnp.exp(decay_log) * step_size)
    head_inputs = conv_inner.astype(jnp.float32).reshape(seqs, local_heads, HEAD_DIM)
    driven = (step_size[:, :, None] * head_inputs)[..., None] * in_maps[:, None, None, :]
    new_state = decay[:, :, None, None] * ssm_state + driven
    readout = (
        jnp.einsum("shpn,sn->shp", new_state, out_maps, precision=lax.Precision.HIGHEST)
        + skip_gain[None, :, None] * head_inputs
    )
    gated = readout.reshape(seqs, local_inner) * jax.nn.silu(gate_input.astype(jnp.float32))
    group_mask = (jnp.arange(GROUPS, dtype=jnp.int32) == group).astype(jnp.float32)
    partial_squares = jnp.sum(gated * gated, axis=1)[:, None] * group_mask[None, :]
    group_squares = lax.psum(partial_squares, "wide")
    own_squares = jnp.sum(group_squares * group_mask[None, :], axis=1, keepdims=True)
    norm_scale = lax.rsqrt(own_squares / (INNER // GROUPS) + epsilon)
    gated_out = (gated * norm_scale * gated_gain.astype(jnp.float32)).astype(jnp.bfloat16)
    mixer_terms = jnp.dot(gated_out, proj_out, preferred_element_type=jnp.float32)
    codes = slot_codes(expert_ids, devices, capacity)
    mixer_slice = lax.psum_scatter(mixer_terms, "wide", scatter_dimension=1, tiled=True)
    hidden_round = (tokens.astype(jnp.float32) + mixer_slice).astype(jnp.bfloat16)
    hidden_slice = lax.optimization_barrier(hidden_round).astype(jnp.float32)
    gain_slice = lax.dynamic_slice_in_dim(moe_gain, device * slice_width, slice_width, 0).astype(
        jnp.float32
    )
    router_slice = lax.dynamic_slice_in_dim(
        router_weight, device * slice_width, slice_width, 0
    ).astype(jnp.float32)
    weighted = hidden_slice * gain_slice
    squares, part_logits = lax.psum(
        (
            jnp.sum(hidden_slice * hidden_slice, axis=1),
            jnp.dot(weighted, router_slice, precision=lax.Precision.HIGHEST),
        ),
        "wide",
    )
    moe_scale = lax.rsqrt(squares[:, None] / WIDTH + epsilon)
    gates = route_gates(part_logits * moe_scale, expert_ids)
    moe_input = (hidden_slice * moe_scale * gain_slice).astype(jnp.bfloat16)
    pick, weigh = slot_tables(codes, gates, devices * capacity)
    sent = (
        jnp.dot(pick, moe_input, preferred_element_type=jnp.float32)
        .astype(jnp.bfloat16)
        .reshape(devices, capacity, slice_width)
    )
    served = expert_rows(
        lax.all_to_all(sent, "wide", split_axis=0, concat_axis=2, tiled=True)[0],
        expert_up[0],
        expert_down[0],
    )
    returned = lax.all_to_all(served[None], "wide", split_axis=2, concat_axis=0, tiled=True)
    moe_slice = jnp.dot(
        weigh.T,
        returned.reshape(devices * capacity, slice_width).astype(jnp.float32),
        precision=lax.Precision.HIGHEST,
    )
    next_hidden = (hidden_slice + moe_slice).astype(jnp.bfloat16)
    return (next_hidden, new_state)


def solution(mesh):
    in_specs = (
        P("group", "wide"),
        P(),
        P(None, None, "wide"),
        P(None, "wide"),
        P(None, "wide"),
        P("group", None, "wide"),
        P("group", None, "wide"),
        P(None, "wide"),
        P(None, "wide"),
        P("wide"),
        P("wide"),
        P("wide"),
        P("wide"),
        P("wide", None),
        P("group", "wide", None, None),
        P(),
        P(),
        P("group", None),
        P("wide", None, None),
        P("wide", None, None),
    )
    out_specs = (P("group", "wide"), P("group", "wide", None, None))
    return jax.shard_map(local, mesh=mesh, in_specs=in_specs, out_specs=out_specs, check_vma=False)
```

profile of v0, /device:TPU:0, one launch (start us, length us, event | category | flops | bytes accessed | tf_op | source)
XLA Modules:
  0.0 292.7 jit_solution(6536486973410003831)
XLA Ops:
  7.3 25.6 %all_gather.6 = bf16[96,2688]{0,1:T(8,128)(2,1)S(1)} all-gather(bf16[96,168]{0,1:T(8,128)(2,1)} %param.20), channel_id=1, replica_groups=mesh['group'=2,'wide'=16] {'wide'}, dimensions={1}, use_global_device_ids=true | all-gather | bytes 548352 | tf_op jit(solution)/shard_map/all_gather | solution.py:84
  33.3 0.7 convert_element_type.109
  34.0 0.7 convert_element_type.120
  34.6 1.8 fusion.24
  36.6 18.5 %all_gather.7 = bf16[96,2048]{1,0:T(8,128)(2,1)S(1)} all-gather(bf16[96,128]{1,0:T(8,128)(2,1)S(1)} %multiply_convert_fusion.3), channel_id=1, replica_groups=mesh['group'=2,'wide'=16] {'wide'}, dimensions={1}, use_global_device_ids=true | all-gather | bytes 417792 | tf_op jit(solution)/shard_map/all_gather | solution.py:99
  55.6 1.2 convolution_convert_fusion.1
  57.9 7.0 %multiply_add_fusion = f32[96,4,64,128]{3,2,1,0:T(8,128)S(1)} fusion(f32[96,4,64,128]{3,2,1,0:T(8,128)} %param.34, f32[96,128]{1,0:T(8,128)S(1)} %get-tuple-element.5, f32[96,4,64]{2,1,0:T(4,128)S(1)} %copy.72, f32[96,4]{1,0:T(8,128)S(1)} %copy.70), kind=kLoop, calls=%fused_computation | loop fusion | flops 9437184 | bytes 25314816 | tf_op jit(solution)/shard_map/add | solution.py:110
  64.9 4.8 %copy-done.1 = f32[96,4,64,128]{3,2,1,0:T(8,128)} copy-done((f32[96,4,64,128]{3,2,1,0:T(8,128)}, f32[96,4,64,128]{3,2,1,0:T(8,128)S(1)}, u32[]{:S(2)}) %copy-start.1) | copy-done | bytes 12582936
  69.7 14.7 %fusion.40 = f32[96,1,4,64]{3,1,2,0:T(1,128)S(1)} fusion(f32[96,4,64,128]{3,2,1,0:T(8,128)S(1)} %multiply_add_fusion, bf16[96,128,1,1]{1,0,2,3:T(8,128)(2,1)S(1)} %get-tuple-element.4), kind=kOutput, calls=%fused_computation.52 | convolution fusion | flops 37748736 | bytes 12705792 | tf_op jit(solution)/shard_map/shpn,sn->shp/dot_general | solution.py:112
  84.9 31.1 %psum.21 = f32[96,8]{0,1:T(8,128)S(1)} all-reduce(f32[96,8]{0,1:T(8,128)S(1)} %broadcast_multiply_fusion.1), channel_id=1, replica_groups=mesh['group'=2,'wide'=16] {'wide'}, use_global_device_ids=true, to_apply=%region_4.5 | all-reduce | flops 768 | bytes 6144 | tf_op jit(solution)/shard_map/psum | solution.py:118
  116.1 1.8 fusion.39
  118.2 1.7 reduce-window.6
  120.4 0.8 dynamic-slice_convert_fusion.1
  121.2 0.6 fusion.4
  121.9 50.8 %reduce-scatter.4.cloned.1.call-done = f32[96,168]{0,1:T(8,128)} async-done(((f32[96,2688]{0,1:T(8,128)}), f32[96,168]{0,1:T(8,128)}) %reduce-scatter.4.cloned.1.call-update) | async-done | bytes 64528
  172.7 0.9 add_convert_fusion
  173.6 0.9 fusion.35
  174.5 30.5 %all-reduce.2 = (f32[96,16]{0,1:T(8,128)S(1)}, f32[96]{0:T(128)S(1)}) all-reduce(f32[96,16]{0,1:T(8,128)S(1)} %fusion.35, f32[96]{0:T(128)S(1)} %fusion.36), channel_id=1, replica_groups=mesh['group'=2,'wide'=16] {'wide'}, use_global_device_ids=true, to_apply=%region_10.11 | all-reduce | flops 1632 | bytes 13056 | tf_op jit(solution)/shard_map/psum | solution.py:134
  205.4 0.6 reshape.115
  206.1 21.2 %all_to_all.30 = bf16[16,96,168]{1,2,0:T(8,128)(2,1)S(1)} all-to-all(bf16[16,96,168]{1,2,0:T(8,128)(2,1)S(1)} %copy.78), channel_id=1, replica_groups=mesh['group'=2,'wide'=16] {'wide'}, dimensions={0} | all-to-all | bytes 1032192 | tf_op jit(solution)/shard_map/all_to_all | solution.py:151
  227.4 6.5 %fusion.8 = bf16[1,96,2688]{2,1,0:T(8,128)(2,1)S(1)} fusion(bf16[1,928,2688]{2,1,0:T(8,128)(2,1)} %param.39, bf16[96,2688]{0,1:T(8,128)(2,1)S(1)} %bitcast.74, bf16[1,2688,928]{1,2,0:T(8,128)(2,1)} %param.38), kind=kOutput, calls=%fused_computation.9 | convolution fusion | flops 958399488 | bytes 11010048 | tf_op jit(solution)/shard_map/dot_general | solution.py:29
  233.9 1.9 copy.80
  236.3 14.9 %reduce.2 = bf16[2688,96]{1,0:T(8,128)(2,1)S(1)} reduce(bf16[2688,1,96]{2,1,0:T(2,128)(2,1)S(1)} %bitcast.70, bf16[]{:T(256)} %broadcast.123), dimensions={1}, to_apply=%bitcast.55.reduce_sub_computation | reduce | bytes 1032194
  251.3 1.9 reshape.122
  253.2 4.5 %all-to-all-start.1 = ((bf16[16,2,8064]{2,1,0:T(2,128)(2,1)}), bf16[16,2,8064]{2,1,0:T(2,128)(2,1)}, u32[]{:S(2)}, u32[]{:S(2)}) async-start(bf16[16,2,8064]{2,1,0:T(2,128)(2,1)} %reshape.122), calls=%async_computation.1 | async-start | bytes 1032192 | tf_op jit(solution)/shard_map/all_to_all | solution.py:155
  258.3 13.3 %all-to-all-done.1 = bf16[16,2,8064]{2,1,0:T(2,128)(2,1)} async-done(((bf16[16,2,8064]{2,1,0:T(2,128)(2,1)}), bf16[16,2,8064]{2,1,0:T(2,128)(2,1)}, u32[]{:S(2)}, u32[]{:S(2)}) %all-to-all-start.1) | async-done | bytes 516128 | tf_op jit(solution)/shard_map/all_to_all | solution.py:155
  271.6 5.0 %reshape.123 = bf16[2688,1,96]{2,1,0:T(2,128)(2,1)S(1)} reshape(bf16[16,2,8064]{2,1,0:T(2,128)(2,1)} %all-to-all-done.1) | data formatting | bytes 1032192
  276.6 2.8 copy.81
  279.4 3.3 %all_to_all.26 = bf16[1,96,16,168]{3,2,1,0:T(8,128)(2,1)S(1)} reshape(bf16[1,96,2688]{2,1,0:T(8,128)(2,1)} %copy.81) | data formatting | bytes 1032192 | tf_op jit(solution)/shard_map/all_to_all | solution.py:155
  282.7 1.2 copy.82
  283.9 0.7 reshape.116
  284.6 1.2 fusion.23
  (72 shorter events, 5.1 us)
Async XLA Ops:
  7.2 108.9 %copy-start = (bf16[256,2688]{1,0:T(8,128)(2,1)S(1)}, bf16[256,2688]{1,0:T(8,128)(2,1)}, u32[]{:S(2)}) copy-start(bf16[256,2688]{1,0:T(8,128)(2,1)} %param.33) | copy-start | bytes 4128772
  7.2 29.3 %copy-start.5 = (bf16[96,3,128]{2,0,1:T(8,128)(2,1)S(1)}, bf16[96,3,128]{2,0,1:T(8,128)(2,1)}, u32[]{:S(2)}) copy-start(bf16[96,3,128]{2,0,1:T(8,128)(2,1)} %param.26) | copy-start | bytes 221188
  7.2 165.5 %reduce-scatter.4.cloned.1.call-start = ((), (), s32[]{:S(2)}) async-start(), calls=%async_computation.3 | async-start | bytes 1462272
  7.3 47.8 %copy-start.2 = (bf16[2688,2,256]{2,1,0:T(2,128)(2,1)S(1)}, bf16[2688,2,256]{2,1,0:T(2,128)(2,1)}, u32[]{:S(2)}) copy-start(bf16[2688,2,256]{2,1,0:T(2,128)(2,1)} %param.22) | copy-start | bytes 8257540
  55.5 1.3 copy-start.7
  55.6 1.3 copy-start.4
  55.6 1.4 copy-start.10
  55.6 1.4 copy-start.9
  55.6 1.4 copy-start.11
  64.9 4.8 %copy-start.1 = (f32[96,4,64,128]{3,2,1,0:T(8,128)}, f32[96,4,64,128]{3,2,1,0:T(8,128)S(1)}, u32[]{:S(2)}) copy-start(f32[96,4,64,128]{3,2,1,0:T(8,128)S(1)} %multiply_add_fusion) | copy-start | bytes 37748740
  69.7 14.8 %copy-start.8 = (f32[4]{0:T(128)S(1)}, f32[4]{0:T(128)}, u32[]{:S(2)}) copy-start(f32[4]{0:T(128)} %param.31) | copy-start | bytes 52
  69.7 46.4 %copy-start.12 = (bf16[256]{0:T(256)(128)(2,1)S(1)}, bf16[256]{0:T(256)(128)(2,1)}, u32[]{:S(2)}) copy-start(bf16[256]{0:T(256)(128)(2,1)} %param.32) | copy-start | bytes 1540
  84.4 33.6 %copy-start.6 = (s32[96,6]{0,1:T(8,128)S(1)}, s32[96,6]{0,1:T(8,128)}, u32[]{:S(2)}) copy-start(s32[96,6]{0,1:T(8,128)} %param.37) | copy-start | bytes 6916
  84.6 88.1 %copy-start.3 = (bf16[96,168]{0,1:T(8,128)(2,1)S(1)}, bf16[96,168]{0,1:T(8,128)(2,1)}, u32[]{:S(2)}) copy-start(bf16[96,168]{0,1:T(8,128)(2,1)} %param.20) | copy-start | bytes 96772
  253.2 18.4 %all-to-all-start.1 = ((bf16[16,2,8064]{2,1,0:T(2,128)(2,1)}), bf16[16,2,8064]{2,1,0:T(2,128)(2,1)}, u32[]{:S(2)}, u32[]{:S(2)}) async-start(bf16[16,2,8064]{2,1,0:T(2,128)(2,1)} %reshape.122), calls=%async_computation.1 | async-start | bytes 1032192 | tf_op jit(solution)/shard_map/all_to_all | solution.py:155
Sparse Core Ops, SparseCore 0:
  118.0 54.5 reduce-scatter.3
where the time goes:
time: 293 us
  blocking collectives  127 us (43%)
  waiting for transfers between devices  64.1 us (22%)
  other arithmetic  29 us (10%)
  matrix products  29 us (10%)
  local copies, waits for them, and re-layouts  24.6 us (8%)
  between operations  14.5 us (5%)
  starting transfers between devices  4.53 us (2%)
    unnamed x2, waiting for transfers between devices  50.8 us
    psum x1, blocking collectives, local(): group_squares = lax.psum(partial_squares, 'wide')  31.1 us
    psum x1, blocking collectives, local(): lax.psum((jnp.sum(hidden_slice * hidden_slice, axis=1), jnp.dot(weighted,...  30.5 us
    all_gather x1, blocking collectives, local(): full_tokens = lax.all_gather(tokens, 'wide', axis=1, tiled=True)  25.6 us
    all_to_all x1, blocking collectives, local(): lax.all_to_all(sent, 'wide', split_axis=0, concat_axis=2, tiled=True)[0]  21.2 us
    all_gather x1, blocking collectives, local(): all_maps = lax.all_gather(conv_maps, 'wide', axis=1, tiled=True)  18.5 us
    unnamed x1, other arithmetic  14.9 us
    dot_general x1, matrix products, local(): jnp.einsum('shpn,sn->shp', new_state, out_maps, precision=lax.Precision.H...  14.7 us
  transfers between devices with their start and end apart: 2, of which 2 were waited for; matrix products, arithmetic and copies ran while one was open for 2% of the time, Pallas kernels for 0%

commit v1 on v0

--- a/solution.py
+++ b/solution.py
@@ -2,6 +2,7 @@
 import jax.numpy as jnp
 from jax import lax
 from jax.sharding import PartitionSpec as P
+from jax.lax import all_gather
 
 WIDTH = 2688
 HEADS = 64
@@ -115,7 +116,7 @@
     gated = readout.reshape(seqs, local_inner) * jax.nn.silu(gate_input.astype(jnp.float32))
     group_mask = (jnp.arange(GROUPS, dtype=jnp.int32) == group).astype(jnp.float32)
     partial_squares = jnp.sum(gated * gated, axis=1)[:, None] * group_mask[None, :]
-    group_squares = lax.psum(partial_squares, "wide")
+    group_squares = all_gather(partial_squares, "wide").sum(axis=0)
     own_squares = jnp.sum(group_squares * group_mask[None, :], axis=1, keepdims=True)
     norm_scale = lax.rsqrt(own_squares / (INNER // GROUPS) + epsilon)
     gated_out = (gated * norm_scale * gated_gain.astype(jnp.float32)).astype(jnp.bfloat16)

time: 293 us -> 281 us (0.959)
  blocking collectives: 127 us -> 115 us
    psum x1 -> x0, blocking collectives: 31.1 us -> none  [local(): group_squares = lax.psum(partial_squares, 'wide')]
    all_gather x0 -> x1, blocking collectives: none -> 18.9 us  [local(): group_squares = all_gather(partial_squares, 'wide').sum(axis=0)]
where the time goes in v1:
time: 281 us
  blocking collectives  115 us (41%)
  waiting for transfers between devices  64.1 us (23%)
  other arithmetic  29 us (10%)
  matrix products  29 us (10%)
  local copies, waits for them, and re-layouts  24.6 us (9%)
  between operations  14.5 us (5%)
  starting transfers between devices  4.53 us (2%)
    unnamed x2, waiting for transfers between devices  50.8 us
    psum x1, blocking collectives, local(): lax.psum((jnp.sum(hidden_slice * hidden_slice, axis=1), jnp.dot(weighted,...  30.5 us
    all_gather x1, blocking collectives, local(): full_tokens = lax.all_gather(tokens, 'wide', axis=1, tiled=True)  25.6 us
    all_to_all x1, blocking collectives, local(): lax.all_to_all(sent, 'wide', split_axis=0, concat_axis=2, tiled=True)[0]  21.2 us
    all_gather x1, blocking collectives, local(): group_squares = all_gather(partial_squares, 'wide').sum(axis=0)  18.9 us
    all_gather x1, blocking collectives, local(): all_maps = lax.all_gather(conv_maps, 'wide', axis=1, tiled=True)  18.5 us
    unnamed x1, other arithmetic  14.9 us
    dot_general x1, matrix products, local(): jnp.einsum('shpn,sn->shp', new_state, out_maps, precision=lax.Precision.H...  14.7 us
  transfers between devices with their start and end apart: 2, of which 2 were waited for; matrix products, arithmetic and copies ran while one was open for 2% of the time, Pallas kernels for 0%

profile of v1, /device:TPU:0, one launch (start us, length us, event | category | flops | bytes accessed | tf_op | source)
XLA Modules:
  0.0 280.5 jit_solution(15201347027252152062)
XLA Ops:
  7.3 25.6 %all_gather.10 = bf16[96,2688]{0,1:T(8,128)(2,1)S(1)} all-gather(bf16[96,168]{0,1:T(8,128)(2,1)} %param.20), channel_id=1, replica_groups=mesh['group'=2,'wide'=16] {'wide'}, dimensions={1}, use_global_device_ids=true | all-gather | bytes 548352 | tf_op jit(solution)/shard_map/all_gather | solution.py:85
  33.3 0.7 convert_element_type.109
  34.0 0.7 convert_element_type.120
  34.6 1.8 fusion.24
  36.6 18.5 %all_gather.11 = bf16[96,2048]{1,0:T(8,128)(2,1)S(1)} all-gather(bf16[96,128]{1,0:T(8,128)(2,1)S(1)} %multiply_convert_fusion.3), channel_id=1, replica_groups=mesh['group'=2,'wide'=16] {'wide'}, dimensions={1}, use_global_device_ids=true | all-gather | bytes 417792 | tf_op jit(solution)/shard_map/all_gather | solution.py:100
  55.6 1.2 convolution_convert_fusion.1
  57.9 7.0 %multiply_add_fusion = f32[96,4,64,128]{3,2,1,0:T(8,128)S(1)} fusion(f32[96,4,64,128]{3,2,1,0:T(8,128)} %param.34, f32[96,128]{1,0:T(8,128)S(1)} %get-tuple-element.5, f32[96,4,64]{2,1,0:T(4,128)S(1)} %copy.88, f32[96,4]{1,0:T(8,128)S(1)} %copy.86), kind=kLoop, calls=%fused_computation | loop fusion | flops 9437184 | bytes 25314816 | tf_op jit(solution)/shard_map/add | solution.py:111
  64.9 4.8 %copy-done.1 = f32[96,4,64,128]{3,2,1,0:T(8,128)} copy-done((f32[96,4,64,128]{3,2,1,0:T(8,128)}, f32[96,4,64,128]{3,2,1,0:T(8,128)S(1)}, u32[]{:S(2)}) %copy-start.1) | copy-done | bytes 12582936
  69.7 14.7 %fusion.40 = f32[96,1,4,64]{3,1,2,0:T(1,128)S(1)} fusion(f32[96,4,64,128]{3,2,1,0:T(8,128)S(1)} %multiply_add_fusion, bf16[96,128,1,1]{1,0,2,3:T(8,128)(2,1)S(1)} %get-tuple-element.4), kind=kOutput, calls=%fused_computation.52 | convolution fusion | flops 37748736 | bytes 12705792 | tf_op jit(solution)/shard_map/shpn,sn->shp/dot_general | solution.py:113
  84.9 18.9 %all_gather.12 = f32[16,96,8]{1,2,0:T(8,128)S(1)} all-gather(f32[1,96,8]{1,2,0:T(8,128)S(1)} %broadcast_multiply_fusion.1), channel_id=1, replica_groups=mesh['group'=2,'wide'=16] {'wide'}, dimensions={0}, use_global_device_ids=true | all-gather | bytes 52224 | tf_op jit(solution)/shard_map/all_gather | solution.py:119
  104.0 1.8 fusion.39
  106.1 1.7 reduce-window.6
  108.3 0.8 dynamic-slice_convert_fusion.1
  109.1 0.6 fusion.4
  109.7 50.8 %reduce-scatter.4.cloned.1.call-done = f32[96,168]{0,1:T(8,128)} async-done(((f32[96,2688]{0,1:T(8,128)}), f32[96,168]{0,1:T(8,128)}) %reduce-scatter.4.cloned.1.call-update) | async-done | bytes 64528
  160.5 0.9 add_convert_fusion
  161.4 0.9 fusion.35
  162.3 30.5 %all-reduce.2 = (f32[96,16]{0,1:T(8,128)S(1)}, f32[96]{0:T(128)S(1)}) all-reduce(f32[96,16]{0,1:T(8,128)S(1)} %fusion.35, f32[96]{0:T(128)S(1)} %fusion.36), channel_id=1, replica_groups=mesh['group'=2,'wide'=16] {'wide'}, use_global_device_ids=true, to_apply=%region_10.11 | all-reduce | flops 1632 | bytes 13056 | tf_op jit(solution)/shard_map/psum | solution.py:135
  193.2 0.6 reshape.156
  193.9 21.2 %all_to_all.30 = bf16[16,96,168]{1,2,0:T(8,128)(2,1)S(1)} all-to-all(bf16[16,96,168]{1,2,0:T(8,128)(2,1)S(1)} %copy.94), channel_id=1, replica_groups=mesh['group'=2,'wide'=16] {'wide'}, dimensions={0} | all-to-all | bytes 1032192 | tf_op jit(solution)/shard_map/all_to_all | solution.py:152
  215.2 6.5 %fusion.8 = bf16[1,96,2688]{2,1,0:T(8,128)(2,1)S(1)} fusion(bf16[1,928,2688]{2,1,0:T(8,128)(2,1)} %param.39, bf16[96,2688]{0,1:T(8,128)(2,1)S(1)} %bitcast.74, bf16[1,2688,928]{1,2,0:T(8,128)(2,1)} %param.38), kind=kOutput, calls=%fused_computation.9 | convolution fusion | flops 958399488 | bytes 11010048 | tf_op jit(solution)/shard_map/dot_general | solution.py:30
  221.7 1.9 copy.96
  224.2 14.9 %reduce.2 = bf16[2688,96]{1,0:T(8,128)(2,1)S(1)} reduce(bf16[2688,1,96]{2,1,0:T(2,128)(2,1)S(1)} %bitcast.70, bf16[]{:T(256)} %broadcast.159), dimensions={1}, to_apply=%bitcast.55.reduce_sub_computation | reduce | bytes 1032194
  239.1 1.9 reshape.163
  241.0 4.5 %all-to-all-start.1 = ((bf16[16,2,8064]{2,1,0:T(2,128)(2,1)}), bf16[16,2,8064]{2,1,0:T(2,128)(2,1)}, u32[]{:S(2)}, u32[]{:S(2)}) async-start(bf16[16,2,8064]{2,1,0:T(2,128)(2,1)} %reshape.163), calls=%async_computation.1 | async-start | bytes 1032192 | tf_op jit(solution)/shard_map/all_to_all | solution.py:156
  246.1 13.3 %all-to-all-done.1 = bf16[16,2,8064]{2,1,0:T(2,128)(2,1)} async-done(((bf16[16,2,8064]{2,1,0:T(2,128)(2,1)}), bf16[16,2,8064]{2,1,0:T(2,128)(2,1)}, u32[]{:S(2)}, u32[]{:S(2)}) %all-to-all-start.1) | async-done | bytes 516128 | tf_op jit(solution)/shard_map/all_to_all | solution.py:156
  259.4 5.0 %reshape.164 = bf16[2688,1,96]{2,1,0:T(2,128)(2,1)S(1)} reshape(bf16[16,2,8064]{2,1,0:T(2,128)(2,1)} %all-to-all-done.1) | data formatting | bytes 1032192
  264.4 2.8 copy.97
  267.2 3.3 %all_to_all.26 = bf16[1,96,16,168]{3,2,1,0:T(8,128)(2,1)S(1)} reshape(bf16[1,96,2688]{2,1,0:T(8,128)(2,1)} %copy.97) | data formatting | bytes 1032192 | tf_op jit(solution)/shard_map/all_to_all | solution.py:156
  270.5 1.2 copy.98
  271.7 0.7 reshape.157
  272.4 1.2 fusion.23
  (73 shorter events, 5.1 us)
Async XLA Ops:
  7.2 96.8 %copy-start = (bf16[256,2688]{1,0:T(8,128)(2,1)S(1)}, bf16[256,2688]{1,0:T(8,128)(2,1)}, u32[]{:S(2)}) copy-start(bf16[256,2688]{1,0:T(8,128)(2,1)} %param.33) | copy-start | bytes 4128772
  7.2 29.3 %copy-start.5 = (bf16[96,3,128]{2,0,1:T(8,128)(2,1)S(1)}, bf16[96,3,128]{2,0,1:T(8,128)(2,1)}, u32[]{:S(2)}) copy-start(bf16[96,3,128]{2,0,1:T(8,128)(2,1)} %param.26) | copy-start | bytes 221188
  7.2 153.3 %reduce-scatter.4.cloned.1.call-start = ((), (), s32[]{:S(2)}) async-start(), calls=%async_computation.3 | async-start | bytes 1462272
  7.3 47.8 %copy-start.2 = (bf16[2688,2,256]{2,1,0:T(2,128)(2,1)S(1)}, bf16[2688,2,256]{2,1,0:T(2,128)(2,1)}, u32[]{:S(2)}) copy-start(bf16[2688,2,256]{2,1,0:T(2,128)(2,1)} %param.22) | copy-start | bytes 8257540
  55.5 1.3 copy-start.7
  55.6 1.3 copy-start.4
  55.6 1.4 copy-start.10
  55.6 1.4 copy-start.9
  55.6 1.4 copy-start.11
  64.9 4.8 %copy-start.1 = (f32[96,4,64,128]{3,2,1,0:T(8,128)}, f32[96,4,64,128]{3,2,1,0:T(8,128)S(1)}, u32[]{:S(2)}) copy-start(f32[96,4,64,128]{3,2,1,0:T(8,128)S(1)} %multiply_add_fusion) | copy-start | bytes 37748740
  69.7 14.8 %copy-start.8 = (f32[4]{0:T(128)S(1)}, f32[4]{0:T(128)}, u32[]{:S(2)}) copy-start(f32[4]{0:T(128)} %param.31) | copy-start | bytes 52
  69.7 34.3 %copy-start.12 = (bf16[256]{0:T(256)(128)(2,1)S(1)}, bf16[256]{0:T(256)(128)(2,1)}, u32[]{:S(2)}) copy-start(bf16[256]{0:T(256)(128)(2,1)} %param.32) | copy-start | bytes 1540
  84.4 21.4 %copy-start.6 = (s32[96,6]{0,1:T(8,128)S(1)}, s32[96,6]{0,1:T(8,128)}, u32[]{:S(2)}) copy-start(s32[96,6]{0,1:T(8,128)} %param.37) | copy-start | bytes 6916
  84.6 75.9 %copy-start.3 = (bf16[96,168]{0,1:T(8,128)(2,1)S(1)}, bf16[96,168]{0,1:T(8,128)(2,1)}, u32[]{:S(2)}) copy-start(bf16[96,168]{0,1:T(8,128)(2,1)} %param.20) | copy-start | bytes 96772
  241.0 18.4 %all-to-all-start.1 = ((bf16[16,2,8064]{2,1,0:T(2,128)(2,1)}), bf16[16,2,8064]{2,1,0:T(2,128)(2,1)}, u32[]{:S(2)}, u32[]{:S(2)}) async-start(bf16[16,2,8064]{2,1,0:T(2,128)(2,1)} %reshape.163), calls=%async_computation.1 | async-start | bytes 1032192 | tf_op jit(solution)/shard_map/all_to_all | solution.py:156
Sparse Core Ops, SparseCore 0:
  105.9 54.5 reduce-scatter.3
